TPU v7x, 128 devices: a whole 4x4x4 slice. The times are simulated.
128 devices in a mesh: mod: 16 (over x, y_hi, core), sp: 8 (over y_lo, z).
Axes of the slice: x: 4, y: 4 (y_hi: 2, y_lo: 2; y = y_hi * 2 + y_lo), z: 4, core: 2. Of those that a mesh axis runs over, the one named last changes fastest.
Arguments:
- images: bfloat16 [16, 512, 64, 256], P('mod', None, 'sp'), may hold values from -6 to 6
- conv_first: bfloat16 [16, 256, 256], P('mod'), may hold values from -0.375 to 0.375
- conv_second: bfloat16 [16, 4096, 256], P('mod'), may hold values from -0.09375 to 0.09375
- project: bfloat16 [16, 256, 512], P('mod'), may hold values from -0.375 to 0.375
- whiten: bfloat16 [16, 512, 256], P('mod'), may hold values from -0.25 to 0.25
- valid_mask: int32 [16, 512, 16, 4], P('mod', None, 'sp'), may hold values 0 or 1
- scene_index: int32 [512], replicated, may hold values from 0 to 63
Outputs:
- target: float32 [512, 256], P('sp')
- grad_view: bfloat16 [16, 512, 256], P('mod', 'sp')
- grad_whiten: float32 [16, 512, 256], P('mod', 'sp')
Inputs may be any that keep to these rules, and one draw needn't show every extreme that they name: `valid_mask`: 1 where a pixel of the encoded map is cloud-free.
All inputs are finite; a program needn't handle non-finite values. No bound on the sum of `valid_mask` on one device may be relied on, other than what follows from the above.
Results may differ from a plain program's by a relative error of at most 0.028.
Values may be sent and summed in bfloat16 or wider, within the bound.
No kernel may reach another device: no remote copies, remote signals or barrier semaphores. Data moves between devices by JAX's collectives and lax.ppermute only.
A program may use at most 192 MiB of HBM per device.

v0:
```python
import jax
import jax.numpy as jnp
from jax import lax
from jax.sharding import PartitionSpec as P

BANDS = 16
CH = 256
SCENES = 64


def extended(x, sides, width):
    for axis, dim in sides:
        size, length = (lax.axis_size(axis), x.shape[dim])
        up = [(i, (i + 1) % size) for i in range(size - 1)]
        down = [(j, i) for i, j in up]
        last = lax.slice_in_dim(x, length - width, length, axis=dim)
        leading = lax.slice_in_dim(x, 0, width, axis=dim)
        before = lax.ppermute(last, axis, up)
        after = lax.ppermute(leading, axis, down)
        x = jnp.concatenate([before, x, after], axis=dim)
    return x


def stride_conv(padded, weight, depth, per_tap):
    count, rows_in, wide = padded.shape
    columns = wide // depth
    sided = jnp.pad(padded, ((0, 0), (0, 0), (depth, depth)))
    paired = sided.reshape(count, rows_in, columns // 2 + 1, 2 * depth)
    joined = jnp.concatenate([paired[:, :, :-1], paired[:, :, 1:]], axis=-1)
    rows_out = (rows_in - 2) // 2
    span = 4 * depth
    taps = [joined[:, offset : offset + 2 * rows_out : 2] for offset in range(4)]
    if per_tap:
        total = jnp.zeros((count * rows_out * (columns // 2), weight.shape[1]), jnp.float32)
        for offset in range(4):
            total = total + jnp.dot(
                taps[offset].reshape(-1, span),
                weight[offset * span : (offset + 1) * span],
                preferred_element_type=jnp.float32,
            )
    else:
        total = jnp.dot(
            jnp.concatenate(taps, axis=-1).reshape(-1, 4 * span),
            weight,
            preferred_element_type=jnp.float32,
        )
    return (
        jnp.maximum(total, 0.0)
        .astype(jnp.bfloat16)
        .reshape(count, rows_out, columns // 2 * weight.shape[1])
    )


def make_view(feat, onehot_rows, scene_sums, counts, whiten_w):
    means = scene_sums / jnp.maximum(counts, 1.0)[:, None]
    panel = (feat - jnp.dot(onehot_rows, means, precision=lax.Precision.HIGHEST)).astype(
        jnp.bfloat16
    )
    raw = jnp.dot(panel, whiten_w, preferred_element_type=jnp.float32)
    scale = 1.0 / jnp.sqrt(jnp.mean(raw * raw, axis=-1, keepdims=True) + 1e-05)
    return (panel, scale, (raw * scale).astype(jnp.bfloat16))


def on_device(images, conv_first, conv_second, project, whiten, valid_mask, scene_index):
    samples = images.shape[1]
    share = samples // lax.axis_size("sp")
    first_row = lax.axis_index("sp") * share
    padded = extended(images[0], (("sp", 1),), 1)
    first = stride_conv(padded, conv_first[0], BANDS, False)
    widened = extended(first, (("sp", 1),), 1)
    second = stride_conv(widened, conv_second[0], CH, True)
    pixels = second.reshape(samples, -1, CH)
    mask_rows = valid_mask[0].reshape(samples, -1).astype(jnp.bfloat16)
    cells = pixels.shape[1] * lax.axis_size("sp")
    pooled_part = (
        jnp.einsum("npc,np->nc", pixels, mask_rows, preferred_element_type=jnp.float32) / cells
    )
    pooled_rows = lax.psum_scatter(pooled_part, "sp", scatter_dimension=0, tiled=True)
    onehot = (scene_index[:, None] == jnp.arange(SCENES, dtype=jnp.int32)[None, :]).astype(
        jnp.float32
    )
    counts = jnp.sum(onehot, axis=0)
    project_w = project[0]
    whiten_w = whiten[0]
    feat = jnp.dot(pooled_rows.astype(jnp.bfloat16), project_w, preferred_element_type=jnp.float32)
    onehot_rows = lax.dynamic_slice_in_dim(onehot, first_row, share, 0)
    local_sums = jnp.dot(onehot_rows.T, feat, precision=lax.Precision.HIGHEST)
    scene_sums = lax.psum(local_sums, "sp")
    panel_rows, scale_rows, view_rows = make_view(feat, onehot_rows, scene_sums, counts, whiten_w)
    view = lax.all_gather(view_rows, "sp", axis=0, tiled=True)
    width = view.shape[1]
    eye = jnp.eye(width, dtype=jnp.float32)
    total = lax.psum(view.astype(jnp.float32).astype(jnp.bfloat16), "mod").astype(jnp.float32)
    piece = lax.all_gather(view[None], "mod", axis=0, tiled=True)
    blocks = jnp.einsum("nk,pnl->pkl", view, piece, preferred_element_type=jnp.float32) / samples
    piece_rows = lax.dynamic_slice_in_dim(piece, first_row, share, 1).astype(jnp.float32)
    coupling = jnp.einsum("pnl,pkl->nk", piece_rows, blocks - eye, precision=lax.Precision.HIGHEST)
    mean_view = total / lax.axis_size("mod")
    gram = jnp.dot(mean_view.T, mean_view, precision=lax.Precision.HIGHEST) / samples + 0.001 * eye
    lower = jnp.linalg.cholesky(gram)
    mean_rows = lax.dynamic_slice_in_dim(mean_view, first_row, share, 0)
    target_rows = jax.scipy.linalg.solve_triangular(lower, mean_rows.T, lower=True).T
    view_f = view_rows.astype(jnp.float32)
    grad_full = view_f - target_rows + coupling
    inner = jnp.mean(grad_full * view_f, axis=-1, keepdims=True)
    grad_raw = ((grad_full - view_f * inner) * scale_rows).astype(jnp.bfloat16)
    grad_w = lax.psum_scatter(
        jnp.dot(panel_rows.T, grad_raw, preferred_element_type=jnp.float32).astype(jnp.bfloat16),
        "sp",
        scatter_dimension=0,
        tiled=True,
    ).astype(jnp.float32)
    return (target_rows, grad_full.astype(jnp.bfloat16)[None], grad_w[None])


def solution(mesh):
    placed = (
        P("mod", None, "sp", None),
        P("mod", None, None),
        P("mod", None, None),
        P("mod", None, None),
        P("mod", None, None),
        P("mod", None, "sp", None),
        P(),
    )
    return jax.shard_map(
        on_device,
        mesh=mesh,
        in_specs=placed,
        out_specs=(P("sp", None), P("mod", "sp", None), P("mod", "sp", None)),
        check_vma=False,
    )
```

profile of v0, /device:TPU:0, one launch (start us, length us, event | category | flops | bytes accessed | tf_op | source)
XLA Modules:
  0.0 805.1 jit_solution(15705632569282844667)
XLA Ops:
  7.2 3.0 copy.29
  10.3 3.9 collective-permute-start
  14.3 1.3 collective-permute-start.1
  15.6 4.2 collective-permute-done
  19.8 4.3 collective-permute-done.1
  24.1 0.3 fusion.16
  24.4 0.6 fusion.75
  25.0 0.7 pad_maximum_fusion.2
  25.7 1.0 fusion.74
  26.7 3.6 pad_maximum_fusion.1
  30.3 14.7 %copy.30 = bf16[512,4,8,256]{3,2,1,0:T(8,128)(2,1)} copy(bf16[512,4,8,256]{0,3,2,1:T(8,128)(2,1)} %pad_maximum_fusion.1) | data formatting | bytes 16777216 | tf_op jit(solution)/shard_map/concatenate | solution.py:43
  45.0 9.0 %fusion.1 = bf16[16384,256]{1,0:T(8,128)(2,1)} fusion(bf16[16384,256]{1,0:T(8,128)(2,1)} %bitcast.98, bf16[1,256,256]{2,1,0:T(8,128)(2,1)S(1)} %copy-done.4), kind=kOutput, calls=%fused_computation.7 | convolution fusion | flops 2155872256 | bytes 16908288 | tf_op jit(solution)/shard_map/dot_general | solution.py:42
  54.0 14.6 %reshape.81 = bf16[512,4,2048]{2,1,0:T(4,128)(2,1)} reshape(bf16[16384,256]{1,0:T(8,128)(2,1)} %fusion.1) | data formatting | bytes 16777216 | tf_op jit(solution)/shard_map/reshape | solution.py:50
  68.5 13.7 %copy.31 = bf16[512,4,2048]{0,2,1:T(8,128)(2,1)} copy(bf16[512,4,2048]{2,1,0:T(4,128)(2,1)} %reshape.81) | data formatting | bytes 16777216 | tf_op jit(solution)/shard_map/reshape | solution.py:50
  82.2 4.6 fusion.73
  86.8 3.8 collective-permute-start.2
  90.5 1.3 collective-permute-start.3
  92.1 42.4 %collective-permute-done.2 = bf16[512,1,2048]{0,2,1:T(8,128)(2,1)S(1)} collective-permute-done((bf16[512,1,2048]{0,2,1:T(8,128)(2,1)}, bf16[512,1,2048]{0,2,1:T(8,128)(2,1)S(1)}, u32[]{:S(2)}, u32[]{:S(2)}) %collective-permute-start.2) | collective-permute-done | bytes 2097184 | tf_op jit(solution)/shard_map/ppermute | solution.py:18
  134.5 4.2 collective-permute-done.3
  138.7 11.7 %fusion.6 = bf16[512,6,2560]{0,2,1:T(8,128)(2,1)S(1)} fusion(bf16[512,1,2048]{0,2,1:T(8,128)(2,1)} %collective-permute-done.3, bf16[512,4,2048]{0,2,1:T(8,128)(2,1)} %copy.31, bf16[512,1,2048]{0,2,1:T(8,128)(2,1)S(1)} %collective-permute-done.2), kind=kLoop, calls=%fused_computation.12 | loop fusion | flops 94371840 | bytes 28311552 | tf_op jit(solution)/shard_map/concatenate | solution.py:20
  150.4 8.6 %fusion.72 = (bf16[512,6,4,512]{0,3,2,1:T(8,128)(2,1)}, bf16[512,6,4,512]{0,3,2,1:T(8,128)(2,1)}) fusion(bf16[512,6,5,512]{0,3,2,1:T(8,128)(2,1)S(1)} %bitcast.97), kind=kLoop, calls=%fused_computation.121 | loop fusion | bytes 50331648 | tf_op jit(solution)/shard_map/slice | solution.py:29
  159.0 20.2 %pad_maximum_fusion = bf16[512,6,4,1024]{0,3,2,1:T(8,128)(2,1)} fusion(bf16[512,6,4,512]{0,3,2,1:T(8,128)(2,1)} %get-tuple-element.26, bf16[512,6,4,512]{0,3,2,1:T(8,128)(2,1)} %get-tuple-element.25), kind=kLoop, calls=%fused_computation.5 | loop fusion | flops 50331648 | bytes 50331648 | tf_op jit(solution)/shard_map/concatenate | solution.py:29
  179.2 22.9 %fusion.71 = (bf16[512,2,4,1024]{0,3,2,1:T(8,128)(2,1)}, bf16[512,2,4,1024]{0,3,2,1:T(8,128)(2,1)}, bf16[512,2,4,1024]{0,3,2,1:T(8,128)(2,1)}, bf16[512,2,4,1024]{0,3,2,1:T(8,128)(2,1)}) fusion(bf16[512,6,4,1024]{0,3,2,1:T(8,128)(2,1)} %pad_maximum_fusion), kind=kLoop, calls=%fused_computation.120 | loop fusion | bytes 67108864 | tf_op jit(solution)/shard_map/slice | solution.py:32
  202.1 14.9 %copy.34 = bf16[512,2,4,1024]{3,2,1,0:T(4,128)(2,1)} copy(bf16[512,2,4,1024]{0,3,2,1:T(8,128)(2,1)} %get-tuple-element.24) | data formatting | bytes 16777216 | tf_op jit(solution)/shard_map/slice | solution.py:32
  217.0 12.6 %reshape.83 = bf16[4096,1024]{1,0:T(8,128)(2,1)} reshape(bf16[512,2,4,1024]{3,2,1,0:T(4,128)(2,1)} %copy.34) | data formatting | bytes 16777216 | tf_op jit(solution)/shard_map/reshape | solution.py:37
  229.5 14.9 %copy.35 = bf16[512,2,4,1024]{3,2,1,0:T(4,128)(2,1)} copy(bf16[512,2,4,1024]{0,3,2,1:T(8,128)(2,1)} %get-tuple-element.23) | data formatting | bytes 16777216 | tf_op jit(solution)/shard_map/slice | solution.py:32
  244.4 12.5 %reshape.84 = bf16[4096,1024]{1,0:T(8,128)(2,1)} reshape(bf16[512,2,4,1024]{3,2,1,0:T(4,128)(2,1)} %copy.35) | data formatting | bytes 16777216 | tf_op jit(solution)/shard_map/reshape | solution.py:37
  256.9 14.9 %copy.36 = bf16[512,2,4,1024]{3,2,1,0:T(4,128)(2,1)} copy(bf16[512,2,4,1024]{0,3,2,1:T(8,128)(2,1)} %get-tuple-element.22) | data formatting | bytes 16777216 | tf_op jit(solution)/shard_map/slice | solution.py:32
  271.8 12.6 %reshape.85 = bf16[4096,1024]{1,0:T(8,128)(2,1)} reshape(bf16[512,2,4,1024]{3,2,1,0:T(4,128)(2,1)} %copy.36) | data formatting | bytes 16777216 | tf_op jit(solution)/shard_map/reshape | solution.py:37
  284.4 14.9 %copy.37 = bf16[512,2,4,1024]{3,2,1,0:T(4,128)(2,1)} copy(bf16[512,2,4,1024]{0,3,2,1:T(8,128)(2,1)} %get-tuple-element.21) | data formatting | bytes 16777216 | tf_op jit(solution)/shard_map/slice | solution.py:32
  299.3 13.1 %reshape.86 = bf16[4096,1024]{1,0:T(8,128)(2,1)} reshape(bf16[512,2,4,1024]{3,2,1,0:T(4,128)(2,1)} %copy.37) | data formatting | bytes 16777216 | tf_op jit(solution)/shard_map/reshape | solution.py:37
  312.4 6.0 fusion.28
  318.4 6.0 convolution_add_fusion.2
  324.4 4.6 convolution_add_fusion.1
  329.0 7.6 fusion.17
  336.6 0.8 bitcast_multiply_fusion
  337.7 41.9 %reduce-scatter.3.cloned.1.call-done = f32[64,256]{1,0:T(8,128)} async-done(((f32[512,256]{1,0:T(8,128)}), f32[64,256]{1,0:T(8,128)}) %reduce-scatter.3.cloned.1.call-update) | async-done | bytes 65552 | tf_op jit(solution)/shard_map/reduce_scatter | solution.py:78
  379.6 1.0 fusion.40
  380.6 0.9 fusion.62
  381.6 73.5 %all-reduce.6.cloned.1.call-done = f32[64,512]{1,0:T(8,128)} async-done(((f32[64,512]{1,0:T(8,128)}), f32[64,512]{1,0:T(8,128)}) %all-reduce.6.cloned.1.call-update) | async-done | bytes 131088 | tf_op jit(solution)/shard_map/psum | solution.py:88
  455.0 1.2 fusion.21
  456.6 30.5 %all_gather.6 = bf16[512,256]{1,0:T(8,128)(2,1)} all-gather(bf16[64,256]{1,0:T(8,128)(2,1)S(1)} %multiply_convert_fusion), channel_id=1, replica_groups=mesh['mod'=16,'sp'=8] {'sp'}, dimensions={0}, use_global_device_ids=true | all-gather | bytes 294912 | tf_op jit(solution)/shard_map/all_gather | solution.py:90
  487.2 54.9 %all-gather.3.cloned.1.call-done = bf16[8192,256]{1,0:T(8,128)(2,1)} async-done(((bf16[512,256]{1,0:T(8,128)(2,1)}), bf16[8192,256]{1,0:T(8,128)(2,1)}) %all-gather.3.cloned.1.call-update) | async-done | bytes 4194320 | tf_op jit(solution)/shard_map/all_gather | solution.py:94
  542.1 5.5 fusion.36
  547.6 0.6 all-reduce.8.cloned.1.call-update
  548.5 139.4 %all-reduce.8.cloned.1.call-done = bf16[512,256]{1,0:T(8,128)(2,1)} async-done(((bf16[512,256]{1,0:T(8,128)(2,1)}), bf16[512,256]{1,0:T(8,128)(2,1)}) %all-reduce.8.cloned.1.call-update) | async-done | bytes 262160 | tf_op jit(solution)/shard_map/psum | solution.py:93
  687.9 2.0 convolution_multiply_fusion
  690.2 11.7 %cholesky.49 = f32[128,128]{1,0:T(8,128)S(1)} custom-call(f32[128,128]{1,0:T(8,128)S(1)} %cholesky.115), custom_call_target="Cholesky" | custom-call | tf_op jit(solution)/shard_map/jit(cholesky)/cholesky | solution.py:100
  702.0 9.8 %custom-call.15 = f32[1,128,128]{1,2,0:T(8,128)S(1)} custom-call(f32[1,128,128]{2,1,0:T(8,128)S(1)} %get-tuple-element.42), custom_call_target="InvertDiagBlocksLowerTriangular" | custom-call | tf_op jit(solution)/shard_map/jit(cholesky)/cholesky | solution.py:100
  712.0 0.3 convolution_subtract_fusion.1
  712.3 11.7 %cholesky.103 = f32[128,128]{1,0:T(8,128)S(1)} custom-call(f32[128,128]{1,0:T(8,128)S(1)} %convolution_subtract_fusion.1), custom_call_target="Cholesky" | custom-call | tf_op jit(solution)/shard_map/jit(cholesky)/cholesky | solution.py:100
  724.0 0.6 compare_reduce_fusion
  726.1 4.2 while.1
  726.3 0.6 fusion.92
  726.9 1.4 bitcast_dynamic-update-slice_fusion.2
  728.3 0.6 fusion.92
  728.9 1.4 bitcast_dynamic-update-slice_fusion.2
  730.3 19.7 %custom-call.16 = f32[2,128,128]{1,2,0:T(8,128)S(1)} custom-call(f32[2,128,128]{2,1,0:T(8,128)S(1)} %get-tuple-element.10), custom_call_target="InvertDiagBlocksLowerTriangular" | custom-call | tf_op jit(solution)/shard_map/jit(_solve_triangular)/triangular_solve | solution.py:102
  749.9 1.0 convert_multiply_fusion
  751.6 4.3 fusion.23
  755.9 0.7 fusion.45
  756.6 1.0 convolution_convert_fusion
  757.7 39.3 %reduce-scatter.5.cloned.1.call-done = bf16[64,256]{1,0:T(8,128)(2,1)} async-done(((bf16[512,256]{1,0:T(8,128)(2,1)}), bf16[64,256]{1,0:T(8,128)(2,1)}) %reduce-scatter.5.cloned.1.call-update) | async-done | bytes 32784 | tf_op jit(solution)/shard_map/reduce_scatter | solution.py:107
  797.0 1.4 bitcast_convert_fusion
  (59 shorter events, 2.5 us)
Async XLA Ops:
  7.2 372.4 %copy-start = (bf16[1,256,512]{2,1,0:T(8,128)(2,1)S(1)}, bf16[1,256,512]{2,1,0:T(8,128)(2,1)}, u32[]{:S(2)}) copy-start(bf16[1,256,512]{2,1,0:T(8,128)(2,1)} %param.10) | copy-start | bytes 786436
  7.2 372.4 %reduce-scatter.3.cloned.1.call-start = ((), (), s32[]{:S(2)}) async-start(), calls=%async_computation.2 | async-start | bytes 589824 | tf_op jit(solution)/shard_map/reduce_scatter | solution.py:78
  10.3 9.5 %collective-permute-start = (bf16[512,1,256]{0,2,1:T(8,128)(2,1)S(1)}, bf16[512,1,256]{0,2,1:T(8,128)(2,1)S(1)}, u32[]{:S(2)}, u32[]{:S(2)}) collective-permute-start(bf16[512,1,256]{0,2,1:T(8,128)(2,1)S(1)} %get-tuple-element.35), channel_id=1, source_target_pairs={{0,1},{1,2},{2,3},{3,4},{4,5},{5,6},{6,7},{8,9},{9,10},{10,11},{11... | collective-permute-start | bytes 786440 | tf_op jit(solution)/shard_map/ppermute | solution.py:18
  14.3 9.8 %collective-permute-start.1 = (bf16[512,1,256]{0,2,1:T(8,128)(2,1)S(1)}, bf16[512,1,256]{0,2,1:T(8,128)(2,1)S(1)}, u32[]{:S(2)}, u32[]{:S(2)}) collective-permute-start(bf16[512,1,256]{0,2,1:T(8,128)(2,1)S(1)} %get-tuple-element.36), channel_id=1, source_target_pairs={{1,0},{2,1},{3,2},{4,3},{5,4},{6,5},{7,6},{9,8},{10,9},{11,10},{12... | collective-permute-start | bytes 786440 | tf_op jit(solution)/shard_map/ppermute | solution.py:19
  30.3 14.7 %copy-start.4 = (bf16[1,256,256]{2,1,0:T(8,128)(2,1)S(1)}, bf16[1,256,256]{2,1,0:T(8,128)(2,1)}, u32[]{:S(2)}) copy-start(bf16[1,256,256]{2,1,0:T(8,128)(2,1)} %param.8) | copy-start | bytes 393220
  82.2 9.6 %copy-start.5 = (s32[1,512,2,4]{1,3,2,0:T(4,128)S(1)}, s32[1,512,2,4]{1,3,2,0:T(4,128)}, u32[]{:S(2)}) copy-start(s32[1,512,2,4]{1,3,2,0:T(4,128)} %param.12) | copy-start | bytes 49156
  86.8 47.7 %collective-permute-start.2 = (bf16[512,1,2048]{0,2,1:T(8,128)(2,1)}, bf16[512,1,2048]{0,2,1:T(8,128)(2,1)S(1)}, u32[]{:S(2)}, u32[]{:S(2)}) collective-permute-start(bf16[512,1,2048]{0,2,1:T(8,128)(2,1)} %get-tuple-element.27), channel_id=1, source_target_pairs={{0,1},{1,2},{2,3},{3,4},{4,5},{5,6},{6,7},{8,9},{9,10},{10,11},{11... | collective-permute-start | bytes 6291464 | tf_op jit(solution)/shard_map/ppermute | solution.py:18
  90.5 48.2 %collective-permute-start.3 = (bf16[512,1,2048]{0,2,1:T(8,128)(2,1)}, bf16[512,1,2048]{0,2,1:T(8,128)(2,1)}, u32[]{:S(2)}, u32[]{:S(2)}) collective-permute-start(bf16[512,1,2048]{0,2,1:T(8,128)(2,1)} %get-tuple-element.28), channel_id=1, source_target_pairs={{1,0},{2,1},{3,2},{4,3},{5,4},{6,5},{7,6},{9,8},{10,9},{11,10},{12... | collective-permute-start | bytes 6291464 | tf_op jit(solution)/shard_map/ppermute | solution.py:19
  299.3 13.1 %copy-start.1 = (bf16[1,4096,256]{2,1,0:T(8,128)(2,1)S(1)}, bf16[1,4096,256]{2,1,0:T(8,128)(2,1)}, u32[]{:S(2)}) copy-start(bf16[1,4096,256]{2,1,0:T(8,128)(2,1)} %param.9) | copy-start | bytes 6291460
  312.4 12.0 %slice-start = ((s8[8388608]{0:T(1024)(128)(4,1)}), s8[4194304]{0:T(1024)(128)(4,1)S(1)}, s32[]{:S(2)}) async-start(s8[8388608]{0:T(1024)(128)(4,1)} %bitcast.99), calls=%async_computation.7 | async-start | bytes 8388608
  318.4 6.0 slice-start.1
  329.0 8.6 %copy-start.6 = (s32[512]{0:T(512)S(1)}, s32[512]{0:T(512)}, u32[]{:S(2)}) copy-start(s32[512]{0:T(512)} %param.13) | copy-start | bytes 6148
  329.0 127.3 %copy-start.3 = (bf16[1,512,256]{2,1,0:T(8,128)(2,1)S(1)}, bf16[1,512,256]{2,1,0:T(8,128)(2,1)}, u32[]{:S(2)}) copy-start(bf16[1,512,256]{2,1,0:T(8,128)(2,1)} %param.11) | copy-start | bytes 786436
  337.5 117.5 %all-reduce.6.cloned.1.call-start = ((), (), s32[]{:S(2)}) async-start(), calls=%async_computation.3 | async-start | bytes 262144 | tf_op jit(solution)/shard_map/psum | solution.py:88
  381.5 160.6 %all-gather.3.cloned.1.call-start = ((), (), s32[]{:S(2)}) async-start(), calls=%async_computation.6 | async-start | bytes 4456448 | tf_op jit(solution)/shard_map/all_gather | solution.py:94
  547.6 140.4 %all-reduce.8.cloned.1.call-start = ((), (), s32[]{:S(2)}) async-start(), calls=%async_computation.4 | async-start | bytes 524288 | tf_op jit(solution)/shard_map/psum | solution.py:93
  548.1 248.9 %reduce-scatter.5.cloned.1.call-start = ((), (), s32[]{:S(2)}) async-start(), calls=%async_computation.5 | async-start | bytes 294912 | tf_op jit(solution)/shard_map/reduce_scatter | solution.py:107
  751.6 46.8 %copy-start.2 = (f32[64,256]{1,0:T(8,128)}, f32[64,256]{1,0:T(8,128)S(1)}, u32[]{:S(2)}) copy-start(f32[64,256]{1,0:T(8,128)S(1)} %maximum_bitcast_fusion) | copy-start | bytes 196612
Sparse Core Ops, SparseCore 0:
  337.6 41.8 reduce-scatter.2
  382.0 72.9 all-reduce.5
  487.3 54.7 all-gather.2
  550.5 137.3 all-reduce.7
  757.8 39.1 reduce-scatter.4
where the time goes:
time: 817 us; the launch traced here: 805 us
  waiting for transfers between devices  405 us (50%)
  local copies, waits for them, and re-layouts  199 us (24%)
  other arithmetic  94.3 us (12%)
  matrix products  50.4 us (6%)
  blocking collectives  30.5 us (4%)
  between operations  15.7 us (2%)
  starting transfers between devices  10.6 us (1%)
    psum x1, waiting for transfers between devices, on_device(): lax.psum(view.astype(jnp.float32).astype(jnp.bfloat16), 'mod')  139 us
    slice x6, local copies, waits for them, and re-layouts, stride_conv(): taps = [joined[:, offset:offset + 2 * rows_out:2] for offset in range(4)]  83.5 us
    psum x1, waiting for transfers between devices, on_device(): scene_sums = lax.psum(local_sums, 'sp')  73.5 us
    all_gather x1, waiting for transfers between devices, on_device(): piece = lax.all_gather(view[None], 'mod', axis=0, tiled=True)  54.9 us
    reshape x4, local copies, waits for them, and re-layouts, stride_conv(): taps[offset].reshape(-1, span)  50.7 us
    ppermute x2, waiting for transfers between devices, extended(): before = lax.ppermute(last, axis, up)  46.6 us
    reduce_scatter x1, waiting for transfers between devices, on_device(): lax.psum_scatter(pooled_part, 'sp', scatter_dimension=0, tiled=True)  41.9 us
    reduce_scatter x1, waiting for transfers between devices, on_device(): lax.psum_scatter(jnp.dot(panel_rows.T, grad_raw, preferred_element_type=j...  39.3 us
  transfers between devices with their start and end apart: 9, of which 9 were waited for; matrix products, arithmetic and copies ran while one was open for 0% of the time, Pallas kernels for 0%

commit v1 on v0

--- a/solution.py
+++ b/solution.py
@@ -85,7 +85,8 @@
     feat = jnp.dot(pooled_rows.astype(jnp.bfloat16), project_w, preferred_element_type=jnp.float32)
     onehot_rows = lax.dynamic_slice_in_dim(onehot, first_row, share, 0)
     local_sums = jnp.dot(onehot_rows.T, feat, precision=lax.Precision.HIGHEST)
-    scene_sums = lax.psum(local_sums, "sp")
+    parts = lax.all_gather(local_sums, "sp", axis=0, tiled=False)
+    scene_sums = parts.sum(axis=0)
     panel_rows, scale_rows, view_rows = make_view(feat, onehot_rows, scene_sums, counts, whiten_w)
     view = lax.all_gather(view_rows, "sp", axis=0, tiled=True)
     width = view.shape[1]

time: 817 us -> 782 us (0.957)
  waiting for transfers between devices: 405 us -> 369 us
    psum x1 -> x0, waiting for transfers between devices: 73.5 us -> none  [on_device(): scene_sums = lax.psum(local_sums, 'sp')]
    all_gather x0 -> x1, waiting for transfers between devices: none -> 37.7 us  [on_device(): parts = lax.all_gather(local_sums, 'sp', axis=0, tiled=False)]
where the time goes in v1:
time: 782 us; the launch traced here: 770 us
  waiting for transfers between devices  369 us (47%)
  local copies, waits for them, and re-layouts  199 us (25%)
  other arithmetic  95.6 us (12%)
  matrix products  49.5 us (6%)
  blocking collectives  30.6 us (4%)
  between operations  15.7 us (2%)
  starting transfers between devices  10.6 us (1%)
    psum x1, waiting for transfers between devices, on_device(): lax.psum(view.astype(jnp.float32).astype(jnp.bfloat16), 'mod')  140 us
    slice x6, local copies, waits for them, and re-layouts, stride_conv(): taps = [joined[:, offset:offset + 2 * rows_out:2] for offset in range(4)]  83.5 us
    all_gather x1, waiting for transfers between devices, on_device(): piece = lax.all_gather(view[None], 'mod', axis=0, tiled=True)  54.9 us
    reshape x4, local copies, waits for them, and re-layouts, stride_conv(): taps[offset].reshape(-1, span)  50.7 us
    ppermute x2, waiting for transfers between devices, extended(): before = lax.ppermute(last, axis, up)  46.6 us
    reduce_scatter x1, waiting for transfers between devices, on_device(): lax.psum_scatter(pooled_part, 'sp', scatter_dimension=0, tiled=True)  42 us
    reduce_scatter x1, waiting for transfers between devices, on_device(): lax.psum_scatter(jnp.dot(panel_rows.T, grad_raw, preferred_element_type=j...  39.3 us
    all_gather x1, waiting for transfers between devices, on_device(): parts = lax.all_gather(local_sums, 'sp', axis=0, tiled=False)  37.7 us
  transfers between devices with their start and end apart: 9, of which 9 were waited for; matrix products, arithmetic and copies ran while one was open for 0% of the time, Pallas kernels for 0%

profile of v1, /device:TPU:0, one launch (start us, length us, event | category | flops | bytes accessed | tf_op | source)
XLA Modules:
  0.0 770.2 jit_solution(16180472594324560484)
XLA Ops:
  7.2 3.0 copy.29
  10.3 3.9 collective-permute-start
  14.3 1.3 collective-permute-start.1
  15.6 4.2 collective-permute-done
  19.8 4.3 collective-permute-done.1
  24.1 0.3 fusion.16
  24.4 0.6 fusion.75
  25.0 0.7 pad_maximum_fusion.2
  25.7 1.0 fusion.74
  26.7 3.6 pad_maximum_fusion.1
  30.3 14.7 %copy.30 = bf16[512,4,8,256]{3,2,1,0:T(8,128)(2,1)} copy(bf16[512,4,8,256]{0,3,2,1:T(8,128)(2,1)} %pad_maximum_fusion.1) | data formatting | bytes 16777216 | tf_op jit(solution)/shard_map/concatenate | solution.py:43
  45.0 9.0 %fusion.1 = bf16[16384,256]{1,0:T(8,128)(2,1)} fusion(bf16[16384,256]{1,0:T(8,128)(2,1)} %bitcast.99, bf16[1,256,256]{2,1,0:T(8,128)(2,1)S(1)} %copy-done.4), kind=kOutput, calls=%fused_computation.7 | convolution fusion | flops 2155872256 | bytes 16908288 | tf_op jit(solution)/shard_map/dot_general | solution.py:42
  54.0 14.6 %reshape.81 = bf16[512,4,2048]{2,1,0:T(4,128)(2,1)} reshape(bf16[16384,256]{1,0:T(8,128)(2,1)} %fusion.1) | data formatting | bytes 16777216 | tf_op jit(solution)/shard_map/reshape | solution.py:50
  68.5 13.7 %copy.31 = bf16[512,4,2048]{0,2,1:T(8,128)(2,1)} copy(bf16[512,4,2048]{2,1,0:T(4,128)(2,1)} %reshape.81) | data formatting | bytes 16777216 | tf_op jit(solution)/shard_map/reshape | solution.py:50
  82.2 4.6 fusion.73
  86.8 3.8 collective-permute-start.2
  90.5 1.3 collective-permute-start.3
  92.1 42.4 %collective-permute-done.2 = bf16[512,1,2048]{0,2,1:T(8,128)(2,1)S(1)} collective-permute-done((bf16[512,1,2048]{0,2,1:T(8,128)(2,1)}, bf16[512,1,2048]{0,2,1:T(8,128)(2,1)S(1)}, u32[]{:S(2)}, u32[]{:S(2)}) %collective-permute-start.2) | collective-permute-done | bytes 2097184 | tf_op jit(solution)/shard_map/ppermute | solution.py:18
  134.5 4.2 collective-permute-done.3
  138.7 11.7 %fusion.6 = bf16[512,6,2560]{0,2,1:T(8,128)(2,1)S(1)} fusion(bf16[512,1,2048]{0,2,1:T(8,128)(2,1)} %collective-permute-done.3, bf16[512,4,2048]{0,2,1:T(8,128)(2,1)} %copy.31, bf16[512,1,2048]{0,2,1:T(8,128)(2,1)S(1)} %collective-permute-done.2), kind=kLoop, calls=%fused_computation.12 | loop fusion | flops 94371840 | bytes 28311552 | tf_op jit(solution)/shard_map/concatenate | solution.py:20
  150.4 8.6 %fusion.72 = (bf16[512,6,4,512]{0,3,2,1:T(8,128)(2,1)}, bf16[512,6,4,512]{0,3,2,1:T(8,128)(2,1)}) fusion(bf16[512,6,5,512]{0,3,2,1:T(8,128)(2,1)S(1)} %bitcast.98), kind=kLoop, calls=%fused_computation.121 | loop fusion | bytes 50331648 | tf_op jit(solution)/shard_map/slice | solution.py:29
  159.0 20.2 %pad_maximum_fusion = bf16[512,6,4,1024]{0,3,2,1:T(8,128)(2,1)} fusion(bf16[512,6,4,512]{0,3,2,1:T(8,128)(2,1)} %get-tuple-element.26, bf16[512,6,4,512]{0,3,2,1:T(8,128)(2,1)} %get-tuple-element.25), kind=kLoop, calls=%fused_computation.5 | loop fusion | flops 50331648 | bytes 50331648 | tf_op jit(solution)/shard_map/concatenate | solution.py:29
  179.2 22.9 %fusion.71 = (bf16[512,2,4,1024]{0,3,2,1:T(8,128)(2,1)}, bf16[512,2,4,1024]{0,3,2,1:T(8,128)(2,1)}, bf16[512,2,4,1024]{0,3,2,1:T(8,128)(2,1)}, bf16[512,2,4,1024]{0,3,2,1:T(8,128)(2,1)}) fusion(bf16[512,6,4,1024]{0,3,2,1:T(8,128)(2,1)} %pad_maximum_fusion), kind=kLoop, calls=%fused_computation.120 | loop fusion | bytes 67108864 | tf_op jit(solution)/shard_map/slice | solution.py:32
  202.1 14.9 %copy.34 = bf16[512,2,4,1024]{3,2,1,0:T(4,128)(2,1)} copy(bf16[512,2,4,1024]{0,3,2,1:T(8,128)(2,1)} %get-tuple-element.24) | data formatting | bytes 16777216 | tf_op jit(solution)/shard_map/slice | solution.py:32
  217.0 12.6 %reshape.83 = bf16[4096,1024]{1,0:T(8,128)(2,1)} reshape(bf16[512,2,4,1024]{3,2,1,0:T(4,128)(2,1)} %copy.34) | data formatting | bytes 16777216 | tf_op jit(solution)/shard_map/reshape | solution.py:37
  229.5 14.9 %copy.35 = bf16[512,2,4,1024]{3,2,1,0:T(4,128)(2,1)} copy(bf16[512,2,4,1024]{0,3,2,1:T(8,128)(2,1)} %get-tuple-element.23) | data formatting | bytes 16777216 | tf_op jit(solution)/shard_map/slice | solution.py:32
  244.4 12.5 %reshape.84 = bf16[4096,1024]{1,0:T(8,128)(2,1)} reshape(bf16[512,2,4,1024]{3,2,1,0:T(4,128)(2,1)} %copy.35) | data formatting | bytes 16777216 | tf_op jit(solution)/shard_map/reshape | solution.py:37
  256.9 14.9 %copy.36 = bf16[512,2,4,1024]{3,2,1,0:T(4,128)(2,1)} copy(bf16[512,2,4,1024]{0,3,2,1:T(8,128)(2,1)} %get-tuple-element.22) | data formatting | bytes 16777216 | tf_op jit(solution)/shard_map/slice | solution.py:32
  271.8 12.6 %reshape.85 = bf16[4096,1024]{1,0:T(8,128)(2,1)} reshape(bf16[512,2,4,1024]{3,2,1,0:T(4,128)(2,1)} %copy.36) | data formatting | bytes 16777216 | tf_op jit(solution)/shard_map/reshape | solution.py:37
  284.4 14.9 %copy.37 = bf16[512,2,4,1024]{3,2,1,0:T(4,128)(2,1)} copy(bf16[512,2,4,1024]{0,3,2,1:T(8,128)(2,1)} %get-tuple-element.21) | data formatting | bytes 16777216 | tf_op jit(solution)/shard_map/slice | solution.py:32
  299.3 13.1 %reshape.86 = bf16[4096,1024]{1,0:T(8,128)(2,1)} reshape(bf16[512,2,4,1024]{3,2,1,0:T(4,128)(2,1)} %copy.37) | data formatting | bytes 16777216 | tf_op jit(solution)/shard_map/reshape | solution.py:37
  312.4 6.0 fusion.28
  318.4 6.0 convolution_add_fusion.2
  324.4 4.6 convolution_add_fusion.1
  329.0 7.6 fusion.17
  336.6 0.8 bitcast_multiply_fusion
  337.6 42.0 %reduce-scatter.3.cloned.1.call-done = f32[64,256]{1,0:T(8,128)} async-done(((f32[512,256]{1,0:T(8,128)}), f32[64,256]{1,0:T(8,128)}) %reduce-scatter.3.cloned.1.call-update) | async-done | bytes 65552 | tf_op jit(solution)/shard_map/reduce_scatter | solution.py:78
  379.6 1.0 fusion.40
  380.6 0.9 fusion.62
  381.7 37.7 %all-gather.5.cloned.1.call-done = f32[512,512]{1,0:T(8,128)} async-done(((f32[64,512]{1,0:T(8,128)}), f32[512,512]{1,0:T(8,128)}) %all-gather.5.cloned.1.call-update) | async-done | bytes 1048592 | tf_op jit(solution)/shard_map/all_gather | solution.py:88
  419.4 1.3 reduce_sum.36
  420.7 0.3 fusion.21
  421.4 30.6 %all_gather.14 = bf16[512,256]{1,0:T(8,128)(2,1)} all-gather(bf16[64,256]{1,0:T(8,128)(2,1)S(1)} %multiply_convert_fusion), channel_id=1, replica_groups=mesh['mod'=16,'sp'=8] {'sp'}, dimensions={0}, use_global_device_ids=true | all-gather | bytes 294912 | tf_op jit(solution)/shard_map/all_gather | solution.py:91
  452.0 54.9 %all-gather.7.cloned.1.call-done = bf16[8192,256]{1,0:T(8,128)(2,1)} async-done(((bf16[512,256]{1,0:T(8,128)(2,1)}), bf16[8192,256]{1,0:T(8,128)(2,1)}) %all-gather.7.cloned.1.call-update) | async-done | bytes 4194320 | tf_op jit(solution)/shard_map/all_gather | solution.py:95
  506.9 5.5 fusion.36
  512.4 0.6 all-reduce.5.cloned.1.call-update
  513.3 139.6 %all-reduce.5.cloned.1.call-done = bf16[512,256]{1,0:T(8,128)(2,1)} async-done(((bf16[512,256]{1,0:T(8,128)(2,1)}), bf16[512,256]{1,0:T(8,128)(2,1)}) %all-reduce.5.cloned.1.call-update) | async-done | bytes 262160 | tf_op jit(solution)/shard_map/psum | solution.py:94
  653.0 2.0 convolution_multiply_fusion
  655.2 11.7 %cholesky.49 = f32[128,128]{1,0:T(8,128)S(1)} custom-call(f32[128,128]{1,0:T(8,128)S(1)} %cholesky.115), custom_call_target="Cholesky" | custom-call | tf_op jit(solution)/shard_map/jit(cholesky)/cholesky | solution.py:101
  667.0 9.8 %custom-call.15 = f32[1,128,128]{1,2,0:T(8,128)S(1)} custom-call(f32[1,128,128]{2,1,0:T(8,128)S(1)} %get-tuple-element.42), custom_call_target="InvertDiagBlocksLowerTriangular" | custom-call | tf_op jit(solution)/shard_map/jit(cholesky)/cholesky | solution.py:101
  677.3 11.7 %cholesky.103 = f32[128,128]{1,0:T(8,128)S(1)} custom-call(f32[128,128]{1,0:T(8,128)S(1)} %convolution_subtract_fusion.1), custom_call_target="Cholesky" | custom-call | tf_op jit(solution)/shard_map/jit(cholesky)/cholesky | solution.py:101
  689.0 0.6 compare_reduce_fusion
  691.1 4.2 while.1
  691.3 0.6 fusion.92
  691.9 1.4 bitcast_dynamic-update-slice_fusion.2
  693.3 0.6 fusion.92
  693.9 1.4 bitcast_dynamic-update-slice_fusion.2
  695.3 19.7 %custom-call.16 = f32[2,128,128]{1,2,0:T(8,128)S(1)} custom-call(f32[2,128,128]{2,1,0:T(8,128)S(1)} %get-tuple-element.10), custom_call_target="InvertDiagBlocksLowerTriangular" | custom-call | tf_op jit(solution)/shard_map/jit(_solve_triangular)/triangular_solve | solution.py:103
  715.0 1.0 convert_multiply_fusion
  716.7 4.3 fusion.23
  720.9 0.7 fusion.45
  721.7 1.0 convolution_convert_fusion
  722.7 39.3 %reduce-scatter.5.cloned.1.call-done = bf16[64,256]{1,0:T(8,128)(2,1)} async-done(((bf16[512,256]{1,0:T(8,128)(2,1)}), bf16[64,256]{1,0:T(8,128)(2,1)}) %reduce-scatter.5.cloned.1.call-update) | async-done | bytes 32784 | tf_op jit(solution)/shard_map/reduce_scatter | solution.py:108
  762.0 1.4 bitcast_convert_fusion
  (60 shorter events, 2.8 us)
Async XLA Ops:
  7.2 372.4 %copy-start = (bf16[1,256,512]{2,1,0:T(8,128)(2,1)S(1)}, bf16[1,256,512]{2,1,0:T(8,128)(2,1)}, u32[]{:S(2)}) copy-start(bf16[1,256,512]{2,1,0:T(8,128)(2,1)} %param.10) | copy-start | bytes 786436
  7.2 372.4 %reduce-scatter.3.cloned.1.call-start = ((), (), s32[]{:S(2)}) async-start(), calls=%async_computation.2 | async-start | bytes 589824 | tf_op jit(solution)/shard_map/reduce_scatter | solution.py:78
  10.3 9.5 %collective-permute-start = (bf16[512,1,256]{0,2,1:T(8,128)(2,1)S(1)}, bf16[512,1,256]{0,2,1:T(8,128)(2,1)S(1)}, u32[]{:S(2)}, u32[]{:S(2)}) collective-permute-start(bf16[512,1,256]{0,2,1:T(8,128)(2,1)S(1)} %get-tuple-element.35), channel_id=1, source_target_pairs={{0,1},{1,2},{2,3},{3,4},{4,5},{5,6},{6,7},{8,9},{9,10},{10,11},{11... | collective-permute-start | bytes 786440 | tf_op jit(solution)/shard_map/ppermute | solution.py:18
  14.3 9.8 %collective-permute-start.1 = (bf16[512,1,256]{0,2,1:T(8,128)(2,1)S(1)}, bf16[512,1,256]{0,2,1:T(8,128)(2,1)S(1)}, u32[]{:S(2)}, u32[]{:S(2)}) collective-permute-start(bf16[512,1,256]{0,2,1:T(8,128)(2,1)S(1)} %get-tuple-element.36), channel_id=1, source_target_pairs={{1,0},{2,1},{3,2},{4,3},{5,4},{6,5},{7,6},{9,8},{10,9},{11,10},{12... | collective-permute-start | bytes 786440 | tf_op jit(solution)/shard_map/ppermute | solution.py:19
  30.3 14.7 %copy-start.4 = (bf16[1,256,256]{2,1,0:T(8,128)(2,1)S(1)}, bf16[1,256,256]{2,1,0:T(8,128)(2,1)}, u32[]{:S(2)}) copy-start(bf16[1,256,256]{2,1,0:T(8,128)(2,1)} %param.8) | copy-start | bytes 393220
  82.2 9.6 %copy-start.5 = (s32[1,512,2,4]{1,3,2,0:T(4,128)S(1)}, s32[1,512,2,4]{1,3,2,0:T(4,128)}, u32[]{:S(2)}) copy-start(s32[1,512,2,4]{1,3,2,0:T(4,128)} %param.12) | copy-start | bytes 49156
  86.8 47.7 %collective-permute-start.2 = (bf16[512,1,2048]{0,2,1:T(8,128)(2,1)}, bf16[512,1,2048]{0,2,1:T(8,128)(2,1)S(1)}, u32[]{:S(2)}, u32[]{:S(2)}) collective-permute-start(bf16[512,1,2048]{0,2,1:T(8,128)(2,1)} %get-tuple-element.27), channel_id=1, source_target_pairs={{0,1},{1,2},{2,3},{3,4},{4,5},{5,6},{6,7},{8,9},{9,10},{10,11},{11... | collective-permute-start | bytes 6291464 | tf_op jit(solution)/shard_map/ppermute | solution.py:18
  90.5 48.2 %collective-permute-start.3 = (bf16[512,1,2048]{0,2,1:T(8,128)(2,1)}, bf16[512,1,2048]{0,2,1:T(8,128)(2,1)}, u32[]{:S(2)}, u32[]{:S(2)}) collective-permute-start(bf16[512,1,2048]{0,2,1:T(8,128)(2,1)} %get-tuple-element.28), channel_id=1, source_target_pairs={{1,0},{2,1},{3,2},{4,3},{5,4},{6,5},{7,6},{9,8},{10,9},{11,10},{12... | collective-permute-start | bytes 6291464 | tf_op jit(solution)/shard_map/ppermute | solution.py:19
  299.3 13.1 %copy-start.1 = (bf16[1,4096,256]{2,1,0:T(8,128)(2,1)S(1)}, bf16[1,4096,256]{2,1,0:T(8,128)(2,1)}, u32[]{:S(2)}) copy-start(bf16[1,4096,256]{2,1,0:T(8,128)(2,1)} %param.9) | copy-start | bytes 6291460
  312.4 12.0 %slice-start = ((s8[8388608]{0:T(1024)(128)(4,1)}), s8[4194304]{0:T(1024)(128)(4,1)S(1)}, s32[]{:S(2)}) async-start(s8[8388608]{0:T(1024)(128)(4,1)} %bitcast.100), calls=%async_computation.7 | async-start | bytes 8388608
  318.4 6.0 slice-start.1
  329.0 8.6 %copy-start.6 = (s32[512]{0:T(512)S(1)}, s32[512]{0:T(512)}, u32[]{:S(2)}) copy-start(s32[512]{0:T(512)} %param.13) | copy-start | bytes 6148
  329.0 92.0 %copy-start.3 = (bf16[1,512,256]{2,1,0:T(8,128)(2,1)S(1)}, bf16[1,512,256]{2,1,0:T(8,128)(2,1)}, u32[]{:S(2)}) copy-start(bf16[1,512,256]{2,1,0:T(8,128)(2,1)} %param.11) | copy-start | bytes 786436
  337.5 81.8 %all-gather.5.cloned.1.call-start = ((), (), s32[]{:S(2)}) async-start(), calls=%async_computation.5 | async-start | bytes 1179648 | tf_op jit(solution)/shard_map/all_gather | solution.py:88
  381.5 125.4 %all-gather.7.cloned.1.call-start = ((), (), s32[]{:S(2)}) async-start(), calls=%async_computation.6 | async-start | bytes 4456448 | tf_op jit(solution)/shard_map/all_gather | solution.py:95
  512.4 140.6 %all-reduce.5.cloned.1.call-start = ((), (), s32[]{:S(2)}) async-start(), calls=%async_computation.3 | async-start | bytes 524288 | tf_op jit(solution)/shard_map/psum | solution.py:94
  512.9 249.1 %reduce-scatter.5.cloned.1.call-start = ((), (), s32[]{:S(2)}) async-start(), calls=%async_computation.4 | async-start | bytes 294912 | tf_op jit(solution)/shard_map/reduce_scatter | solution.py:108
  716.6 46.8 %copy-start.2 = (f32[64,256]{1,0:T(8,128)}, f32[64,256]{1,0:T(8,128)S(1)}, u32[]{:S(2)}) copy-start(f32[64,256]{1,0:T(8,128)S(1)} %maximum_bitcast_fusion) | copy-start | bytes 196612
Sparse Core Ops, SparseCore 0:
  337.6 41.8 reduce-scatter.2
  381.6 37.6 all-gather.4
  452.1 54.7 all-gather.6
  515.3 137.6 all-reduce.4
  722.8 39.1 reduce-scatter.4
